TPU v7x, 32 devices: a whole 2x2x4 slice. The times are simulated.
32 devices in a mesh: sec: 4 (over y, x), term: 8 (over z, core).
Axes of the slice: x: 2, y: 2, z: 4, core: 2. Of those that a mesh axis runs over, the one named last changes fastest.
Arguments:
- theta: bfloat16 [4, 896, 896], P('sec', 'term'), may hold values from -6 to 6
- left_env: bfloat16 [16, 4, 896, 896], P('term', 'sec'), may hold values from -2 to 2
- right_env: bfloat16 [16, 4, 896, 896], P('term', 'sec'), may hold values from -2 to 2
- term_shift: int32 [16], P('term'), may hold values from -1 to 1
- term_on: int32 [16, 4], P('term', 'sec'), may hold values 0 or 1
- block_rows: int32 [4], P('sec'), may hold values from 224 to 896
- block_cols: int32 [4], P('sec'), may hold values from 224 to 896
Outputs:
- basis_last: float32 [4, 896, 896], P('sec', 'term')
- alphas: float32 [2], replicated
- betas: float32 [2], replicated
All inputs are finite; a program needn't handle non-finite values. No bound on the sum of `term_on` on one device may be relied on, other than what follows from the above.
Results may differ from a plain program's by a relative error of at most 0.0037.
Values may be sent and summed in bfloat16 or wider, within the bound.
No kernel may reach another device: no remote copies, remote signals or barrier semaphores. Data moves between devices by JAX's collectives and lax.ppermute only.
A program may use at most 64 MiB of HBM per device.

v0:
```python
import jax
import jax.numpy as jnp
from jax import lax
from jax.sharding import PartitionSpec as P

ITERS = 2
EPS = 1e-06


def extended(block, sides, width):
    for axis, dim in sides:
        count = lax.axis_size(axis)
        forward = [(i, i + 1) for i in range(count - 1)]
        backward = [(target, source) for source, target in forward]
        low = lax.ppermute(
            lax.slice_in_dim(block, block.shape[dim] - width, None, axis=dim), axis, forward
        )
        high = lax.ppermute(lax.slice_in_dim(block, 0, width, axis=dim), axis, backward)
        block = jnp.concatenate([low, block, high], axis=dim)
    return block


def on_device(theta, left_env, right_env, term_shift, term_on, block_rows, block_cols):
    sectors = theta.shape[0]
    row_count = theta.shape[1]
    width = theta.shape[2]
    terms_here = left_env.shape[0]
    full_count = row_count * lax.axis_size("term")
    row_offset = lax.axis_index("term") * row_count
    col_line = jnp.arange(width, dtype=jnp.int32)
    col_mask = (col_line[None, :] < block_cols[:, None]).astype(jnp.float32)
    local_rows = row_offset + jnp.arange(row_count, dtype=jnp.int32)
    row_mask = (local_rows[None, :] < block_rows[:, None]).astype(jnp.float32)
    mask = row_mask[:, :, None] * col_mask[:, None, :]
    on_float = term_on.astype(jnp.float32)
    start = mask * theta.astype(jnp.float32)
    norm_start = lax.psum(jnp.sum(start * start), ("sec", "term"))
    vector = start / jnp.sqrt(norm_start + EPS)
    previous = jnp.zeros_like(vector)
    beta_prev = jnp.float32(0.0)
    alpha_list = []
    beta_list = []
    for step in range(ITERS):
        vector_bf = vector.astype(jnp.bfloat16)
        full_rows = lax.all_gather(vector_bf, "term", axis=1, tiled=True)
        padded = extended(full_rows, (("sec", 0),), 1)
        source_list = [
            lax.dynamic_slice_in_dim(padded, 1 + term_shift[term_index], sectors, 0)
            for term_index in range(terms_here)
        ]
        total = jnp.zeros((full_count, sectors, width), jnp.float32)
        for partial_term_index in range(terms_here):
            left_rows = left_env[partial_term_index]
            product = jnp.einsum(
                "sik,skj->sij",
                left_rows,
                source_list[partial_term_index],
                preferred_element_type=jnp.float32,
            ).astype(jnp.bfloat16)
            result = jnp.einsum(
                "sij,sjk->isk",
                product,
                right_env[partial_term_index],
                preferred_element_type=jnp.float32,
            )
            total = total + on_float[partial_term_index][None, :, None] * result
        row_index = jnp.arange(full_count, dtype=jnp.int32)
        rows_inside = (row_index[:, None] < block_rows[None, :]).astype(jnp.float32)
        total = total * rows_inside[:, :, None] * col_mask[None, :, :]
        summed = lax.psum(total.reshape(full_count, sectors * width), "term")
        scattered = lax.dynamic_slice_in_dim(summed, row_offset, row_count, 0)
        image = scattered.reshape(row_count, sectors, width).transpose(1, 0, 2)
        alpha = lax.psum(jnp.sum(vector * image), ("sec", "term"))
        residual = image - alpha * vector - beta_prev * previous
        beta_square = lax.psum(jnp.sum(residual * residual), ("sec", "term"))
        beta = jnp.sqrt(beta_square + EPS)
        previous = vector
        vector = residual / beta
        beta_prev = beta
        alpha_list.append(alpha)
        beta_list.append(beta)
    return (vector, jnp.stack(alpha_list), jnp.stack(beta_list))


def solution(mesh):
    return jax.shard_map(
        on_device,
        mesh=mesh,
        in_specs=(
            P("sec", "term", None),
            P("term", "sec", None, None),
            P("term", "sec", None, None),
            P("term"),
            P("term", "sec"),
            P("sec"),
            P("sec"),
        ),
        out_specs=(P("sec", "term", None), P(), P()),
        check_vma=False,
    )
```

profile of v0, /device:TPU:0, one launch (start us, length us, event | category | flops | bytes accessed | tf_op | source)
XLA Modules:
  0.0 632.7 jit_solution(16715820950023222964)
XLA Ops:
  7.2 0.0 all-gather.3.cloned.1.call-start
  8.5 1.7 multiply_reduce_fusion.2
  10.2 42.2 %psum.49 = f32[]{:T(128)} all-reduce(f32[]{:T(128)} %multiply_reduce_fusion.2), channel_id=1, replica_groups=mesh['sec'=4,'term'=8] {'sec','term'}, use_global_device_ids=true, to_apply=%region_1.0 | all-reduce | flops 1 | bytes 8 | tf_op jit(solution)/shard_map/psum | solution.py:37
  53.1 1.7 fusion.61
  54.9 0.0 all-gather.3.cloned.1.call-update
  54.9 0.0 all-reduce.3.cloned.1.call-start
  55.0 25.3 %all-gather.3.cloned.1.call-done = bf16[1,896,896]{2,1,0:T(8,128)(2,1)} async-done(((bf16[1,112,896]{2,1,0:T(8,128)(2,1)}), bf16[1,896,896]{2,1,0:T(8,128)(2,1)}) %all-gather.3.cloned.1.call-update) | async-done | bytes 1605648 | tf_op jit(solution)/shard_map/all_gather | solution.py:45
  80.3 0.0 copy-start.1
  80.3 4.7 collective-permute-start
  85.0 1.3 collective-permute-start.1
  86.2 1.3 fusion.63
  90.2 0.7 convert_element_type.60
  90.8 0.6 fusion.64
  91.4 27.4 %collective-permute-done = bf16[1,896,896]{2,1,0:T(8,128)(2,1)} collective-permute-done((bf16[1,896,896]{2,1,0:T(8,128)(2,1)}, bf16[1,896,896]{2,1,0:T(8,128)(2,1)}, u32[]{:S(2)}, u32[]{:S(2)}) %collective-permute-start) | collective-permute-done | bytes 1605664 | tf_op jit(solution)/shard_map/ppermute | solution.py:15
  118.8 2.7 constant_dynamic-update-slice_fusion.2
  121.6 0.0 copy-done.1
  121.6 1.3 constant_dynamic-update-slice_fusion.1
  122.9 32.2 %collective-permute-done.1 = bf16[1,896,896]{2,1,0:T(8,128)(2,1)S(1)} collective-permute-done((bf16[1,896,896]{2,1,0:T(8,128)(2,1)}, bf16[1,896,896]{2,1,0:T(8,128)(2,1)S(1)}, u32[]{:S(2)}, u32[]{:S(2)}) %collective-permute-start.1) | collective-permute-done | bytes 1605664 | tf_op jit(solution)/shard_map/ppermute | solution.py:18
  155.1 1.3 constant_dynamic-update-slice_fusion
  156.4 0.0 copy-start.3
  156.4 8.2 %fusion.13 = f32[896,896]{1,0:T(8,128)} fusion(bf16[2,1,896,896]{3,2,1,0:T(8,128)(2,1)} %param.9, bf16[3,896,896]{2,1,0:T(8,128)(2,1)} %constant_dynamic-update-slice_fusion, s32[]{:T(128)S(6)} %select_n.12, bf16[2,1,896,896]{3,2,1,0:T(8,128)(2,1)} %param.8), kind=kOutput, calls=%fused_computation.19 | convolution fusion | flops 2878095360 | bytes 8028164 | tf_op jit(solution)/shard_map/sij,sjk->isk/dot_general | solution.py:60
  164.6 0.0 copy-done.3
  164.6 10.1 %fusion.3 = f32[896,896]{1,0:T(8,128)} fusion(f32[896,896]{1,0:T(8,128)} %fusion.13, f32[896]{0:T(1024)S(1)} %fusion.50, f32[896]{0:T(1024)S(1)} %fusion.51, f32[]{:T(128)} %bitcast.8, f32[]{:T(128)} %bitcast, bf16[2,1,896,896]{3,2,1,0:T(8,128)(2,1)S(1)} %copy-done.3, bf16[3,896,896]{2,1,0:T(8,128)(2,1)} %constant_dynamic-update-slice_fusion, ...), kind=kOutput, calls=%fused_computation.5 | convolution fusion | flops 2882109440 | bytes 11248644 | tf_op jit(solution)/shard_map/sij,sjk->isk/dot_general | solution.py:60
  174.7 0.0 copy-start
  174.7 0.0 all-reduce.3.cloned.1.call-update
  174.7 0.0 all-gather.5.cloned.1.call-start
  174.8 76.8 %all-reduce.3.cloned.1.call-done = f32[896,896]{1,0:T(8,128)} async-done(((f32[896,896]{1,0:T(8,128)}), f32[896,896]{1,0:T(8,128)}) %all-reduce.3.cloned.1.call-update) | async-done | bytes 3211280 | tf_op jit(solution)/shard_map/psum | solution.py:70
  251.5 0.0 copy-done
  251.5 1.8 fusion.48
  253.3 40.4 %psum.51 = f32[]{:T(128)} all-reduce(f32[]{:T(128)} %fusion.48), channel_id=1, replica_groups=mesh['sec'=4,'term'=8] {'sec','term'}, use_global_device_ids=true, to_apply=%region_4.0 | all-reduce | flops 1 | bytes 8 | tf_op jit(solution)/shard_map/psum | solution.py:73
  293.7 2.4 multiply_reduce_fusion.1
  296.1 39.6 %psum.52 = f32[]{:T(128)} all-reduce(f32[]{:T(128)} %multiply_reduce_fusion.1), channel_id=1, replica_groups=mesh['sec'=4,'term'=8] {'sec','term'}, use_global_device_ids=true, to_apply=%region_6.0 | all-reduce | flops 1 | bytes 8 | tf_op jit(solution)/shard_map/psum | solution.py:75
  336.4 2.5 fusion.60
  338.8 0.0 all-gather.5.cloned.1.call-update
  338.9 0.2 all-reduce.5.cloned.1.call-start
  339.1 26.1 %all-gather.5.cloned.1.call-done = bf16[1,896,896]{2,1,0:T(8,128)(2,1)} async-done(((bf16[1,112,896]{2,1,0:T(8,128)(2,1)}), bf16[1,896,896]{2,1,0:T(8,128)(2,1)}) %all-gather.5.cloned.1.call-update) | async-done | bytes 1605648 | tf_op jit(solution)/shard_map/all_gather | solution.py:45
  365.2 0.0 copy-start.2
  365.2 3.6 collective-permute-start.2
  368.8 1.3 collective-permute-start.3
  370.1 33.6 %collective-permute-done.2 = bf16[1,896,896]{2,1,0:T(8,128)(2,1)S(1)} collective-permute-done((bf16[1,896,896]{2,1,0:T(8,128)(2,1)}, bf16[1,896,896]{2,1,0:T(8,128)(2,1)S(1)}, u32[]{:S(2)}, u32[]{:S(2)}) %collective-permute-start.2) | collective-permute-done | bytes 1605664 | tf_op jit(solution)/shard_map/ppermute | solution.py:15
  403.7 1.3 constant_dynamic-update-slice_fusion.5
  405.0 0.0 copy-done.2
  405.0 1.3 constant_dynamic-update-slice_fusion.4
  406.3 33.6 %collective-permute-done.3 = bf16[1,896,896]{2,1,0:T(8,128)(2,1)S(1)} collective-permute-done((bf16[1,896,896]{2,1,0:T(8,128)(2,1)}, bf16[1,896,896]{2,1,0:T(8,128)(2,1)S(1)}, u32[]{:S(2)}, u32[]{:S(2)}) %collective-permute-start.3) | collective-permute-done | bytes 1605664 | tf_op jit(solution)/shard_map/ppermute | solution.py:18
  439.9 1.3 constant_dynamic-update-slice_fusion.3
  441.2 8.1 %fusion.11 = f32[896,896]{1,0:T(8,128)} fusion(bf16[2,1,896,896]{3,2,1,0:T(8,128)(2,1)} %param.9, bf16[3,896,896]{2,1,0:T(8,128)(2,1)} %constant_dynamic-update-slice_fusion.3, s32[]{:T(128)S(6)} %select_n.12, bf16[2,1,896,896]{3,2,1,0:T(8,128)(2,1)} %param.8), kind=kOutput, calls=%fused_computation.17 | convolution fusion | flops 2878095360 | bytes 8028164 | tf_op jit(solution)/shard_map/sij,sjk->isk/dot_general | solution.py:60
  449.3 10.6 %fusion.1 = f32[896,896]{1,0:T(8,128)} fusion(f32[896,896]{1,0:T(8,128)} %fusion.11, f32[896]{0:T(1024)S(1)} %fusion.50, f32[896]{0:T(1024)S(1)} %fusion.51, f32[]{:T(128)} %bitcast.8, f32[]{:T(128)} %bitcast, bf16[2,1,896,896]{3,2,1,0:T(8,128)(2,1)} %param.9, bf16[3,896,896]{2,1,0:T(8,128)(2,1)} %constant_dynamic-update-slice_fusion.3, s32[]{:T(128)S(6)} %select_n.13, ...), kind=kOutput, calls=%fused_computation.2 | convolution fusion | flops 2882109440 | bytes 11247620 | tf_op jit(solution)/shard_map/sij,sjk->isk/dot_general | solution.py:60
  459.9 0.0 all-reduce.5.cloned.1.call-update
  459.9 76.8 %all-reduce.5.cloned.1.call-done = f32[896,896]{1,0:T(8,128)} async-done(((f32[896,896]{1,0:T(8,128)}), f32[896,896]{1,0:T(8,128)}) %all-reduce.5.cloned.1.call-update) | async-done | bytes 3211280 | tf_op jit(solution)/shard_map/psum | solution.py:70
  536.7 2.5 fusion.46
  539.2 40.4 %psum.54 = f32[]{:T(128)} all-reduce(f32[]{:T(128)} %fusion.46), channel_id=1, replica_groups=mesh['sec'=4,'term'=8] {'sec','term'}, use_global_device_ids=true, to_apply=%region_9.0 | all-reduce | flops 1 | bytes 8 | tf_op jit(solution)/shard_map/psum | solution.py:73
  579.6 3.2 multiply_reduce_fusion
  582.8 39.5 %psum.55 = f32[]{:T(128)} all-reduce(f32[]{:T(128)} %get-tuple-element.3), channel_id=1, replica_groups=mesh['sec'=4,'term'=8] {'sec','term'}, use_global_device_ids=true, to_apply=%region_11.0 | all-reduce | flops 1 | bytes 8 | tf_op jit(solution)/shard_map/psum | solution.py:75
  623.0 0.8 broadcast_divide_fusion
  623.8 0.6 pad_maximum_fusion.1
  624.4 1.7 pad_maximum_fusion
  (3 shorter events, 0.0 us)
Async XLA Ops:
  7.2 73.1 %all-gather.3.cloned.1.call-start = ((), (), s32[]{:S(2)}) async-start(), calls=%async_computation | async-start | bytes 1806336 | tf_op jit(solution)/shard_map/all_gather | solution.py:45
  54.9 196.6 %all-reduce.3.cloned.1.call-start = ((), (), s32[]{:S(2)}) async-start(), calls=%async_computation.1 | async-start | bytes 6422528 | tf_op jit(solution)/shard_map/psum | solution.py:70
  80.3 41.3 %copy-start.1 = (bf16[1,896,896]{2,1,0:T(8,128)(2,1)S(1)}, bf16[1,896,896]{2,1,0:T(8,128)(2,1)}, u32[]{:S(2)}) copy-start(bf16[1,896,896]{2,1,0:T(8,128)(2,1)} %all-gather.3.cloned.1.call-done) | copy-start | bytes 4816900
  80.3 38.6 %collective-permute-start = (bf16[1,896,896]{2,1,0:T(8,128)(2,1)}, bf16[1,896,896]{2,1,0:T(8,128)(2,1)}, u32[]{:S(2)}, u32[]{:S(2)}) collective-permute-start(bf16[1,896,896]{2,1,0:T(8,128)(2,1)} %all-gather.3.cloned.1.call-done), channel_id=1, source_target_pairs={{0,8},{8,16},{16,24},{1,9},{9,17},{17,25},{2,10},{10,18},{18,26},{... | collective-permute-start | bytes 4816904 | tf_op jit(solution)/shard_map/ppermute | solution.py:15
  85.0 70.1 %collective-permute-start.1 = (bf16[1,896,896]{2,1,0:T(8,128)(2,1)}, bf16[1,896,896]{2,1,0:T(8,128)(2,1)S(1)}, u32[]{:S(2)}, u32[]{:S(2)}) collective-permute-start(bf16[1,896,896]{2,1,0:T(8,128)(2,1)} %all-gather.3.cloned.1.call-done), channel_id=1, source_target_pairs={{8,0},{16,8},{24,16},{9,1},{17,9},{25,17},{10,2},{18,10},{26,18},{... | collective-permute-start | bytes 4816904 | tf_op jit(solution)/shard_map/ppermute | solution.py:18
  156.4 8.2 %copy-start.3 = (bf16[2,1,896,896]{3,2,1,0:T(8,128)(2,1)S(1)}, bf16[2,1,896,896]{3,2,1,0:T(8,128)(2,1)}, u32[]{:S(2)}) copy-start(bf16[2,1,896,896]{3,2,1,0:T(8,128)(2,1)} %param.9) | copy-start | bytes 9633796
  174.7 76.8 %copy-start = (bf16[1,112,896]{2,1,0:T(8,128)(2,1)S(1)}, bf16[1,112,896]{2,1,0:T(8,128)(2,1)}, u32[]{:S(2)}) copy-start(bf16[1,112,896]{2,1,0:T(8,128)(2,1)} %param.7) | copy-start | bytes 602116
  174.7 190.4 %all-gather.5.cloned.1.call-start = ((), (), s32[]{:S(2)}) async-start(), calls=%async_computation.2 | async-start | bytes 1806336 | tf_op jit(solution)/shard_map/all_gather | solution.py:45
  338.9 197.9 %all-reduce.5.cloned.1.call-start = ((), (), s32[]{:S(2)}) async-start(), calls=%async_computation.3 | async-start | bytes 6422528 | tf_op jit(solution)/shard_map/psum | solution.py:70
  365.2 39.9 %copy-start.2 = (bf16[1,896,896]{2,1,0:T(8,128)(2,1)S(1)}, bf16[1,896,896]{2,1,0:T(8,128)(2,1)}, u32[]{:S(2)}) copy-start(bf16[1,896,896]{2,1,0:T(8,128)(2,1)} %all-gather.5.cloned.1.call-done) | copy-start | bytes 4816900
  365.2 38.5 %collective-permute-start.2 = (bf16[1,896,896]{2,1,0:T(8,128)(2,1)}, bf16[1,896,896]{2,1,0:T(8,128)(2,1)S(1)}, u32[]{:S(2)}, u32[]{:S(2)}) collective-permute-start(bf16[1,896,896]{2,1,0:T(8,128)(2,1)} %all-gather.5.cloned.1.call-done), channel_id=1, source_target_pairs={{0,8},{8,16},{16,24},{1,9},{9,17},{17,25},{2,10},{10,18},{18,26},{... | collective-permute-start | bytes 4816904 | tf_op jit(solution)/shard_map/ppermute | solution.py:15
  368.8 71.2 %collective-permute-start.3 = (bf16[1,896,896]{2,1,0:T(8,128)(2,1)}, bf16[1,896,896]{2,1,0:T(8,128)(2,1)S(1)}, u32[]{:S(2)}, u32[]{:S(2)}) collective-permute-start(bf16[1,896,896]{2,1,0:T(8,128)(2,1)} %all-gather.5.cloned.1.call-done), channel_id=1, source_target_pairs={{8,0},{16,8},{24,16},{9,1},{17,9},{25,17},{10,2},{18,10},{26,18},{... | collective-permute-start | bytes 4816904 | tf_op jit(solution)/shard_map/ppermute | solution.py:18
Sparse Core Ops, SparseCore 0:
  55.0 25.2 all-gather.2
  174.8 76.6 all-reduce.2
  339.0 26.1 all-gather.4
  460.0 76.6 all-reduce.4
where the time goes:
time: 634 us; the launch traced here: 633 us
  waiting for transfers between devices  332 us (52%)
  blocking collectives  202 us (32%)
  matrix products  36.9 us (6%)
  between operations  19.8 us (3%)
  other arithmetic  19.6 us (3%)
  starting transfers between devices  11.2 us (2%)
  local copies, waits for them, and re-layouts  11.1 us (2%)
    psum x2, waiting for transfers between devices, on_device(): summed = lax.psum(total.reshape(full_count, sectors * width), 'term')  154 us
    psum x2, blocking collectives, on_device(): alpha = lax.psum(jnp.sum(vector * image), ('sec', 'term'))  80.8 us
    psum x2, blocking collectives, on_device(): beta_square = lax.psum(jnp.sum(residual * residual), ('sec', 'term'))  79.1 us
    ppermute x2, waiting for transfers between devices, extended(): lax.ppermute(lax.slice_in_dim(block, 0, width, axis=dim), axis, backward)  65.8 us
    ppermute x2, waiting for transfers between devices, extended(): lax.ppermute(lax.slice_in_dim(block, block.shape[dim] - width, None, axis...  61.1 us
    all_gather x2, waiting for transfers between devices, on_device(): full_rows = lax.all_gather(vector_bf, 'term', axis=1, tiled=True)  51.4 us
    psum x1, blocking collectives, on_device(): norm_start = lax.psum(jnp.sum(start * start), ('sec', 'term'))  42.2 us
    dot_general x4, matrix products, on_device(): jnp.einsum('sij,sjk->isk', product, right_env[partial_term_index], prefer...  36.9 us
  transfers between devices with their start and end apart: 8, of which 8 were waited for; matrix products, arithmetic and copies ran while one was open for 1% of the time, Pallas kernels for 0%

commit v1 on v0

--- a/solution.py
+++ b/solution.py
@@ -5,6 +5,17 @@
 
 ITERS = 2
 EPS = 1e-06
+
+
+def gather_by_hops(shard, axis, dim):
+    size = lax.axis_size(axis)
+    route = [(i, (i + 1) % size) for i in range(size)]
+    parts = [shard]
+    for hop in range(1, size):
+        parts = [lax.ppermute(parts[0], axis, route), *parts]
+    out = jnp.concatenate(parts, axis=dim)
+    offset = (lax.axis_index(axis) + 1) * parts[-1].shape[dim]
+    return jnp.roll(out, offset, axis=dim)
 
 
 def extended(block, sides, width):
@@ -42,7 +53,7 @@
     beta_list = []
     for step in range(ITERS):
         vector_bf = vector.astype(jnp.bfloat16)
-        full_rows = lax.all_gather(vector_bf, "term", axis=1, tiled=True)
+        full_rows = gather_by_hops(vector_bf, "term", 1)
         padded = extended(full_rows, (("sec", 0),), 1)
         source_list = [
             lax.dynamic_slice_in_dim(padded, 1 + term_shift[term_index], sectors, 0)

time: 634 us -> 674 us (1.063)
  waiting for transfers between devices: 332 us -> 370 us
  other arithmetic: 19.6 us -> 29.6 us
  local copies, waits for them, and re-layouts: 11.1 us -> 1.55 us
    ppermute x0 -> x14, waiting for transfers between devices: none -> 97.1 us  [gather_by_hops(): parts = [lax.ppermute(parts[0], axis, route), *parts]]
    ppermute x2, waiting for transfers between devices: 61.1 us -> 0.01 us  [extended(): lax.ppermute(lax.slice_in_dim(block, block.shape[dim] - width, None, axis...]
    psum x2, waiting for transfers between devices: 154 us -> 210 us  [on_device(): summed = lax.psum(total.reshape(full_count, sectors * width), 'term')]
    all_gather x2 -> x0, waiting for transfers between devices: 51.4 us -> none  [on_device(): full_rows = lax.all_gather(vector_bf, 'term', axis=1, tiled=True)]
    concatenate x0 -> x5, other arithmetic: none -> 12 us  [the longest x2 6.66 us: extended(): block = jnp.concatenate([low, block, high], axis=dim)]
  transfers between devices with their start and end apart: 8 -> 20, of which waited for: 8 -> 18; matrix products, arithmetic and copies ran while one was open for 1% -> 0% of each run, Pallas kernels for 0% -> 0%
where the time goes in v1:
time: 674 us; the launch traced here: 673 us
  waiting for transfers between devices  370 us (55%)
  blocking collectives  202 us (30%)
  matrix products  36.1 us (5%)
  other arithmetic  29.6 us (4%)
  between operations  20.3 us (3%)
  starting transfers between devices  13.7 us (2%)
    psum x2, waiting for transfers between devices, on_device(): summed = lax.psum(total.reshape(full_count, sectors * width), 'term')  210 us
    ppermute x14, waiting for transfers between devices, gather_by_hops(): parts = [lax.ppermute(parts[0], axis, route), *parts]  97.1 us
    psum x2, blocking collectives, on_device(): alpha = lax.psum(jnp.sum(vector * image), ('sec', 'term'))  80.7 us
    psum x2, blocking collectives, on_device(): beta_square = lax.psum(jnp.sum(residual * residual), ('sec', 'term'))  79.1 us
    ppermute x2, waiting for transfers between devices, extended(): lax.ppermute(lax.slice_in_dim(block, 0, width, axis=dim), axis, backward)  63.1 us
    psum x1, blocking collectives, on_device(): norm_start = lax.psum(jnp.sum(start * start), ('sec', 'term'))  42.2 us
    dot_general x4, matrix products, on_device(): jnp.einsum('sij,sjk->isk', product, right_env[partial_term_index], prefer...  36.1 us
  transfers between devices with their start and end apart: 20, of which 18 were waited for; matrix products, arithmetic and copies ran while one was open for 0% of the time, Pallas kernels for 0%

profile of v1, /device:TPU:0, one launch (start us, length us, event | category | flops | bytes accessed | tf_op | source)
XLA Modules:
  0.0 672.9 jit_solution(10669873852891290281)
XLA Ops:
  7.2 0.0 all-reduce.3.cloned.1.call-start
  8.5 1.7 multiply_reduce_fusion.2
  10.2 42.2 %psum.49 = f32[]{:T(128)} all-reduce(f32[]{:T(128)} %multiply_reduce_fusion.2), channel_id=1, replica_groups=mesh['sec'=4,'term'=8] {'sec','term'}, use_global_device_ids=true, to_apply=%region_1.0 | all-reduce | flops 1 | bytes 8 | tf_op jit(solution)/shard_map/psum | solution.py:48
  53.1 0.0 copy-start
  53.1 1.1 fusion.63
  54.3 0.1 collective-permute-start
  54.3 6.9 %collective-permute-done = bf16[1,112,896]{2,1,0:T(8,128)(2,1)S(1)} collective-permute-done((bf16[1,112,896]{2,1,0:T(8,128)(2,1)S(1)}, bf16[1,112,896]{2,1,0:T(8,128)(2,1)S(1)}, u32[]{:S(2)}, u32[]{:S(2)}) %collective-permute-start) | collective-permute-done | bytes 200736 | tf_op jit(solution)/shard_map/ppermute | solution.py:15
  61.3 0.0 collective-permute-start.1
  61.3 6.9 %collective-permute-done.1 = bf16[1,112,896]{2,1,0:T(8,128)(2,1)S(1)} collective-permute-done((bf16[1,112,896]{2,1,0:T(8,128)(2,1)S(1)}, bf16[1,112,896]{2,1,0:T(8,128)(2,1)S(1)}, u32[]{:S(2)}, u32[]{:S(2)}) %collective-permute-start.1) | collective-permute-done | bytes 200736 | tf_op jit(solution)/shard_map/ppermute | solution.py:15
  68.2 6.9 %collective-permute-done.2 = bf16[1,112,896]{2,1,0:T(8,128)(2,1)S(1)} collective-permute-done((bf16[1,112,896]{2,1,0:T(8,128)(2,1)S(1)}, bf16[1,112,896]{2,1,0:T(8,128)(2,1)S(1)}, u32[]{:S(2)}, u32[]{:S(2)}) %collective-permute-start.2) | collective-permute-done | bytes 200736 | tf_op jit(solution)/shard_map/ppermute | solution.py:15
  75.1 0.0 collective-permute-start.3
  75.1 6.9 %collective-permute-done.3 = bf16[1,112,896]{2,1,0:T(8,128)(2,1)S(1)} collective-permute-done((bf16[1,112,896]{2,1,0:T(8,128)(2,1)S(1)}, bf16[1,112,896]{2,1,0:T(8,128)(2,1)S(1)}, u32[]{:S(2)}, u32[]{:S(2)}) %collective-permute-start.3) | collective-permute-done | bytes 200736 | tf_op jit(solution)/shard_map/ppermute | solution.py:15
  82.1 0.0 collective-permute-start.4
  82.1 6.9 %collective-permute-done.4 = bf16[1,112,896]{2,1,0:T(8,128)(2,1)S(1)} collective-permute-done((bf16[1,112,896]{2,1,0:T(8,128)(2,1)S(1)}, bf16[1,112,896]{2,1,0:T(8,128)(2,1)S(1)}, u32[]{:S(2)}, u32[]{:S(2)}) %collective-permute-start.4) | collective-permute-done | bytes 200736 | tf_op jit(solution)/shard_map/ppermute | solution.py:15
  89.0 6.9 %collective-permute-done.5 = bf16[1,112,896]{2,1,0:T(8,128)(2,1)S(1)} collective-permute-done((bf16[1,112,896]{2,1,0:T(8,128)(2,1)S(1)}, bf16[1,112,896]{2,1,0:T(8,128)(2,1)S(1)}, u32[]{:S(2)}, u32[]{:S(2)}) %collective-permute-start.5) | collective-permute-done | bytes 200736 | tf_op jit(solution)/shard_map/ppermute | solution.py:15
  96.0 0.0 collective-permute-start.6
  96.0 6.9 %collective-permute-done.6 = bf16[1,112,896]{2,1,0:T(8,128)(2,1)S(1)} collective-permute-done((bf16[1,112,896]{2,1,0:T(8,128)(2,1)S(1)}, bf16[1,112,896]{2,1,0:T(8,128)(2,1)S(1)}, u32[]{:S(2)}, u32[]{:S(2)}) %collective-permute-start.6) | collective-permute-done | bytes 200736 | tf_op jit(solution)/shard_map/ppermute | solution.py:15
  103.1 0.2 constant_dynamic-update-slice_fusion
  103.3 0.0 copy-start.3
  103.3 2.6 fusion.5
  105.9 1.3 collective-permute-start.8
  107.2 6.0 collective-permute-start.7
  113.2 0.6 fusion.65
  116.4 0.6 fusion.66
  117.0 29.1 %collective-permute-done.8 = bf16[1,896,896]{2,1,0:T(8,128)(2,1)S(1)} collective-permute-done((bf16[1,896,896]{2,1,0:T(8,128)(2,1)S(1)}, bf16[1,896,896]{2,1,0:T(8,128)(2,1)S(1)}, u32[]{:S(2)}, u32[]{:S(2)}) %collective-permute-start.8) | collective-permute-done | bytes 1605664 | tf_op jit(solution)/shard_map/ppermute | solution.py:29
  146.0 0.0 collective-permute-done.7
  146.1 4.2 pad_maximum_fusion
  150.2 8.2 %fusion.15 = f32[896,896]{1,0:T(8,128)} fusion(bf16[2,1,896,896]{3,2,1,0:T(8,128)(2,1)} %param.11, bf16[3,896,896]{2,1,0:T(8,128)(2,1)} %pad_maximum_fusion, s32[]{:T(128)S(6)} %select_n.22, bf16[2,1,896,896]{3,2,1,0:T(8,128)(2,1)} %param.10), kind=kOutput, calls=%fused_computation.27 | convolution fusion | flops 2878095360 | bytes 8028164 | tf_op jit(solution)/shard_map/sij,sjk->isk/dot_general | solution.py:71
  158.5 10.1 %fusion.3 = f32[896,896]{1,0:T(8,128)} fusion(f32[896,896]{1,0:T(8,128)} %fusion.15, f32[896]{0:T(1024)S(1)} %fusion.52, f32[896]{0:T(1024)S(1)} %fusion.53, f32[]{:T(128)} %bitcast.8, f32[]{:T(128)} %bitcast, bf16[2,1,896,896]{3,2,1,0:T(8,128)(2,1)S(1)} %copy-done.2, bf16[3,896,896]{2,1,0:T(8,128)(2,1)} %pad_maximum_fusion, s32[]{:T(128)S(6)} %select_n.23, ...), kind=kOutput, calls=%fused_computation.11 | convolution fusion | flops 2882109440 | bytes 11248644 | tf_op jit(solution)/shard_map/sij,sjk->isk/dot_general | solution.py:71
  168.6 0.0 all-reduce.3.cloned.1.call-update
  168.6 0.0 all-reduce.5.cloned.1.call-start
  168.7 104.8 %all-reduce.3.cloned.1.call-done = f32[896,896]{1,0:T(8,128)} async-done(((f32[896,896]{1,0:T(8,128)}), f32[896,896]{1,0:T(8,128)}) %all-reduce.3.cloned.1.call-update) | async-done | bytes 3211280 | tf_op jit(solution)/shard_map/psum | solution.py:81
  273.4 1.8 fusion.50
  275.2 40.4 %psum.51 = f32[]{:T(128)} all-reduce(f32[]{:T(128)} %fusion.50), channel_id=1, replica_groups=mesh['sec'=4,'term'=8] {'sec','term'}, use_global_device_ids=true, to_apply=%region_4.6 | all-reduce | flops 1 | bytes 8 | tf_op jit(solution)/shard_map/psum | solution.py:84
  315.6 2.4 multiply_reduce_fusion.1
  318.0 39.6 %psum.52 = f32[]{:T(128)} all-reduce(f32[]{:T(128)} %multiply_reduce_fusion.1), channel_id=1, replica_groups=mesh['sec'=4,'term'=8] {'sec','term'}, use_global_device_ids=true, to_apply=%region_6.8 | all-reduce | flops 1 | bytes 8 | tf_op jit(solution)/shard_map/psum | solution.py:86
  358.3 1.8 fusion.62
  360.1 0.1 collective-permute-start.9
  360.1 6.9 %collective-permute-done.9 = bf16[1,112,896]{2,1,0:T(8,128)(2,1)S(1)} collective-permute-done((bf16[1,112,896]{2,1,0:T(8,128)(2,1)S(1)}, bf16[1,112,896]{2,1,0:T(8,128)(2,1)S(1)}, u32[]{:S(2)}, u32[]{:S(2)}) %collective-permute-start.9) | collective-permute-done | bytes 200736 | tf_op jit(solution)/shard_map/ppermute | solution.py:15
  367.0 0.0 collective-permute-start.10
  367.0 6.9 %collective-permute-done.10 = bf16[1,112,896]{2,1,0:T(8,128)(2,1)S(1)} collective-permute-done((bf16[1,112,896]{2,1,0:T(8,128)(2,1)S(1)}, bf16[1,112,896]{2,1,0:T(8,128)(2,1)S(1)}, u32[]{:S(2)}, u32[]{:S(2)}) %collective-permute-start.10) | collective-permute-done | bytes 200736 | tf_op jit(solution)/shard_map/ppermute | solution.py:15
  374.0 6.9 %collective-permute-done.11 = bf16[1,112,896]{2,1,0:T(8,128)(2,1)S(1)} collective-permute-done((bf16[1,112,896]{2,1,0:T(8,128)(2,1)S(1)}, bf16[1,112,896]{2,1,0:T(8,128)(2,1)S(1)}, u32[]{:S(2)}, u32[]{:S(2)}) %collective-permute-start.11) | collective-permute-done | bytes 200736 | tf_op jit(solution)/shard_map/ppermute | solution.py:15
  380.9 0.0 collective-permute-start.12
  380.9 6.9 %collective-permute-done.12 = bf16[1,112,896]{2,1,0:T(8,128)(2,1)S(1)} collective-permute-done((bf16[1,112,896]{2,1,0:T(8,128)(2,1)S(1)}, bf16[1,112,896]{2,1,0:T(8,128)(2,1)S(1)}, u32[]{:S(2)}, u32[]{:S(2)}) %collective-permute-start.12) | collective-permute-done | bytes 200736 | tf_op jit(solution)/shard_map/ppermute | solution.py:15
  387.9 6.9 %collective-permute-done.13 = bf16[1,112,896]{2,1,0:T(8,128)(2,1)S(1)} collective-permute-done((bf16[1,112,896]{2,1,0:T(8,128)(2,1)S(1)}, bf16[1,112,896]{2,1,0:T(8,128)(2,1)S(1)}, u32[]{:S(2)}, u32[]{:S(2)}) %collective-permute-start.13) | collective-permute-done | bytes 200736 | tf_op jit(solution)/shard_map/ppermute | solution.py:15
  394.8 6.9 %collective-permute-done.14 = bf16[1,112,896]{2,1,0:T(8,128)(2,1)S(1)} collective-permute-done((bf16[1,112,896]{2,1,0:T(8,128)(2,1)S(1)}, bf16[1,112,896]{2,1,0:T(8,128)(2,1)S(1)}, u32[]{:S(2)}, u32[]{:S(2)}) %collective-permute-start.14) | collective-permute-done | bytes 200736 | tf_op jit(solution)/shard_map/ppermute | solution.py:15
  401.7 0.0 collective-permute-start.15
  401.7 6.9 %collective-permute-done.15 = bf16[1,112,896]{2,1,0:T(8,128)(2,1)S(1)} collective-permute-done((bf16[1,112,896]{2,1,0:T(8,128)(2,1)S(1)}, bf16[1,112,896]{2,1,0:T(8,128)(2,1)S(1)}, u32[]{:S(2)}, u32[]{:S(2)}) %collective-permute-start.15) | collective-permute-done | bytes 200736 | tf_op jit(solution)/shard_map/ppermute | solution.py:15
  408.9 2.6 fusion.4
  411.5 1.3 collective-permute-start.17
  412.8 4.9 collective-permute-start.16
  417.7 34.0 %collective-permute-done.17 = bf16[1,896,896]{2,1,0:T(8,128)(2,1)S(1)} collective-permute-done((bf16[1,896,896]{2,1,0:T(8,128)(2,1)S(1)}, bf16[1,896,896]{2,1,0:T(8,128)(2,1)S(1)}, u32[]{:S(2)}, u32[]{:S(2)}) %collective-permute-start.17) | collective-permute-done | bytes 1605664 | tf_op jit(solution)/shard_map/ppermute | solution.py:29
  451.7 2.5 pad_maximum_fusion.1
  454.1 7.6 %fusion.13 = f32[896,896]{1,0:T(8,128)} fusion(bf16[2,1,896,896]{3,2,1,0:T(8,128)(2,1)S(1)} %copy-done.2, bf16[3,896,896]{2,1,0:T(8,128)(2,1)} %pad_maximum_fusion.1, s32[]{:T(128)S(6)} %select_n.22, bf16[2,1,896,896]{3,2,1,0:T(8,128)(2,1)} %param.10), kind=kOutput, calls=%fused_computation.25 | convolution fusion | flops 2878095360 | bytes 8028164 | tf_op jit(solution)/shard_map/sij,sjk->isk/dot_general | solution.py:71
  461.8 10.1 %fusion.1 = f32[896,896]{1,0:T(8,128)} fusion(f32[896,896]{1,0:T(8,128)} %fusion.13, f32[896]{0:T(1024)S(1)} %fusion.52, f32[896]{0:T(1024)S(1)} %fusion.53, f32[]{:T(128)} %bitcast.8, f32[]{:T(128)} %bitcast, bf16[2,1,896,896]{3,2,1,0:T(8,128)(2,1)S(1)} %copy-done.2, bf16[3,896,896]{2,1,0:T(8,128)(2,1)} %pad_maximum_fusion.1, s32[]{:T(128)S(6)} %select_n.23, ...), kind=kOutput, calls=%fused_computation.8 | convolution fusion | flops 2882109440 | bytes 11248644 | tf_op jit(solution)/shard_map/sij,sjk->isk/dot_general | solution.py:71
  471.9 0.0 all-reduce.5.cloned.1.call-update
  471.9 104.7 %all-reduce.5.cloned.1.call-done = f32[896,896]{1,0:T(8,128)} async-done(((f32[896,896]{1,0:T(8,128)}), f32[896,896]{1,0:T(8,128)}) %all-reduce.5.cloned.1.call-update) | async-done | bytes 3211280 | tf_op jit(solution)/shard_map/psum | solution.py:81
  576.6 2.5 fusion.48
  579.2 40.4 %psum.54 = f32[]{:T(128)} all-reduce(f32[]{:T(128)} %fusion.48), channel_id=1, replica_groups=mesh['sec'=4,'term'=8] {'sec','term'}, use_global_device_ids=true, to_apply=%region_9.11 | all-reduce | flops 1 | bytes 8 | tf_op jit(solution)/shard_map/psum | solution.py:84
  619.5 3.2 multiply_reduce_fusion
  622.7 39.5 %psum.55 = f32[]{:T(128)} all-reduce(f32[]{:T(128)} %get-tuple-element.4), channel_id=1, replica_groups=mesh['sec'=4,'term'=8] {'sec','term'}, use_global_device_ids=true, to_apply=%region_11.13 | all-reduce | flops 1 | bytes 8 | tf_op jit(solution)/shard_map/psum | solution.py:86
  662.9 0.8 broadcast_divide_fusion
  663.7 0.6 pad_maximum_fusion.3
  664.3 1.7 pad_maximum_fusion.2
  (31 shorter events, 0.4 us)
Async XLA Ops:
  7.2 266.3 %all-reduce.3.cloned.1.call-start = ((), (), s32[]{:S(2)}) async-start(), calls=%async_computation | async-start | bytes 6422528 | tf_op jit(solution)/shard_map/psum | solution.py:81
  53.1 50.0 %copy-start = (bf16[1,112,896]{2,1,0:T(8,128)(2,1)S(1)}, bf16[1,112,896]{2,1,0:T(8,128)(2,1)}, u32[]{:S(2)}) copy-start(bf16[1,112,896]{2,1,0:T(8,128)(2,1)} %param.9) | copy-start | bytes 602116
  54.3 7.0 %collective-permute-start = (bf16[1,112,896]{2,1,0:T(8,128)(2,1)S(1)}, bf16[1,112,896]{2,1,0:T(8,128)(2,1)S(1)}, u32[]{:S(2)}, u32[]{:S(2)}) collective-permute-start(bf16[1,112,896]{2,1,0:T(8,128)(2,1)S(1)} %fusion.63), channel_id=1, source_target_pairs={{0,1},{1,2},{2,3},{3,4},{4,5},{5,6},{6,7},{7,0},{8,9},{9,10},{10,1... | collective-permute-start | bytes 602120 | tf_op jit(solution)/shard_map/ppermute | solution.py:15
  61.3 6.9 %collective-permute-start.1 = (bf16[1,112,896]{2,1,0:T(8,128)(2,1)S(1)}, bf16[1,112,896]{2,1,0:T(8,128)(2,1)S(1)}, u32[]{:S(2)}, u32[]{:S(2)}) collective-permute-start(bf16[1,112,896]{2,1,0:T(8,128)(2,1)S(1)} %collective-permute-done), channel_id=1, source_target_pairs={{0,1},{1,2},{2,3},{3,4},{4,5},{5,6},{6,7},{7,0},{8,9},{9,10},{10,1... | collective-permute-start | bytes 602120 | tf_op jit(solution)/shard_map/ppermute | solution.py:15
  68.2 6.9 %collective-permute-start.2 = (bf16[1,112,896]{2,1,0:T(8,128)(2,1)S(1)}, bf16[1,112,896]{2,1,0:T(8,128)(2,1)S(1)}, u32[]{:S(2)}, u32[]{:S(2)}) collective-permute-start(bf16[1,112,896]{2,1,0:T(8,128)(2,1)S(1)} %collective-permute-done.1), channel_id=1, source_target_pairs={{0,1},{1,2},{2,3},{3,4},{4,5},{5,6},{6,7},{7,0},{8,9},{9,10},{10,1... | collective-permute-start | bytes 602120 | tf_op jit(solution)/shard_map/ppermute | solution.py:15
  75.1 6.9 %collective-permute-start.3 = (bf16[1,112,896]{2,1,0:T(8,128)(2,1)S(1)}, bf16[1,112,896]{2,1,0:T(8,128)(2,1)S(1)}, u32[]{:S(2)}, u32[]{:S(2)}) collective-permute-start(bf16[1,112,896]{2,1,0:T(8,128)(2,1)S(1)} %collective-permute-done.2), channel_id=1, source_target_pairs={{0,1},{1,2},{2,3},{3,4},{4,5},{5,6},{6,7},{7,0},{8,9},{9,10},{10,1... | collective-permute-start | bytes 602120 | tf_op jit(solution)/shard_map/ppermute | solution.py:15
  82.1 6.9 %collective-permute-start.4 = (bf16[1,112,896]{2,1,0:T(8,128)(2,1)S(1)}, bf16[1,112,896]{2,1,0:T(8,128)(2,1)S(1)}, u32[]{:S(2)}, u32[]{:S(2)}) collective-permute-start(bf16[1,112,896]{2,1,0:T(8,128)(2,1)S(1)} %collective-permute-done.3), channel_id=1, source_target_pairs={{0,1},{1,2},{2,3},{3,4},{4,5},{5,6},{6,7},{7,0},{8,9},{9,10},{10,1... | collective-permute-start | bytes 602120 | tf_op jit(solution)/shard_map/ppermute | solution.py:15
  89.0 6.9 %collective-permute-start.5 = (bf16[1,112,896]{2,1,0:T(8,128)(2,1)S(1)}, bf16[1,112,896]{2,1,0:T(8,128)(2,1)S(1)}, u32[]{:S(2)}, u32[]{:S(2)}) collective-permute-start(bf16[1,112,896]{2,1,0:T(8,128)(2,1)S(1)} %collective-permute-done.4), channel_id=1, source_target_pairs={{0,1},{1,2},{2,3},{3,4},{4,5},{5,6},{6,7},{7,0},{8,9},{9,10},{10,1... | collective-permute-start | bytes 602120 | tf_op jit(solution)/shard_map/ppermute | solution.py:15
  96.0 6.9 %collective-permute-start.6 = (bf16[1,112,896]{2,1,0:T(8,128)(2,1)S(1)}, bf16[1,112,896]{2,1,0:T(8,128)(2,1)S(1)}, u32[]{:S(2)}, u32[]{:S(2)}) collective-permute-start(bf16[1,112,896]{2,1,0:T(8,128)(2,1)S(1)} %collective-permute-done.5), channel_id=1, source_target_pairs={{0,1},{1,2},{2,3},{3,4},{4,5},{5,6},{6,7},{7,0},{8,9},{9,10},{10,1... | collective-permute-start | bytes 602120 | tf_op jit(solution)/shard_map/ppermute | solution.py:15
  103.3 9.9 %copy-start.1 = (s32[2]{0:T(128)S(1)}, s32[2]{0:T(128)}, u32[]{:S(2)}) copy-start(s32[2]{0:T(128)} %param.12) | copy-start | bytes 28
  103.3 13.1 %copy-start.3 = (s32[2,1]{0,1:T(1,128)S(1)}, s32[2,1]{0,1:T(1,128)}, u32[]{:S(2)}) copy-start(s32[2,1]{0,1:T(1,128)} %param.13) | copy-start | bytes 28
  105.9 40.2 %collective-permute-start.8 = (bf16[1,896,896]{2,1,0:T(8,128)(2,1)S(1)}, bf16[1,896,896]{2,1,0:T(8,128)(2,1)S(1)}, u32[]{:S(2)}, u32[]{:S(2)}) collective-permute-start(bf16[1,896,896]{2,1,0:T(8,128)(2,1)S(1)} %fusion.5), channel_id=1, source_target_pairs={{8,0},{16,8},{24,16},{9,1},{17,9},{25,17},{10,2},{18,10},{26,18},{... | collective-permute-start | bytes 4816904 | tf_op jit(solution)/shard_map/ppermute | solution.py:29
  107.2 38.9 %collective-permute-start.7 = (bf16[1,896,896]{2,1,0:T(8,128)(2,1)S(1)}, bf16[1,896,896]{2,1,0:T(8,128)(2,1)}, u32[]{:S(2)}, u32[]{:S(2)}) collective-permute-start(bf16[1,896,896]{2,1,0:T(8,128)(2,1)S(1)} %fusion.5), channel_id=1, source_target_pairs={{0,8},{8,16},{16,24},{1,9},{9,17},{17,25},{2,10},{10,18},{18,26},{... | collective-permute-start | bytes 4816904 | tf_op jit(solution)/shard_map/ppermute | solution.py:26
  150.2 8.2 %copy-start.2 = (bf16[2,1,896,896]{3,2,1,0:T(8,128)(2,1)S(1)}, bf16[2,1,896,896]{3,2,1,0:T(8,128)(2,1)}, u32[]{:S(2)}) copy-start(bf16[2,1,896,896]{3,2,1,0:T(8,128)(2,1)} %param.11) | copy-start | bytes 9633796
  168.6 408.0 %all-reduce.5.cloned.1.call-start = ((), (), s32[]{:S(2)}) async-start(), calls=%async_computation.1 | async-start | bytes 6422528 | tf_op jit(solution)/shard_map/psum | solution.py:81
  360.1 7.0 %collective-permute-start.9 = (bf16[1,112,896]{2,1,0:T(8,128)(2,1)S(1)}, bf16[1,112,896]{2,1,0:T(8,128)(2,1)S(1)}, u32[]{:S(2)}, u32[]{:S(2)}) collective-permute-start(bf16[1,112,896]{2,1,0:T(8,128)(2,1)S(1)} %fusion.62), channel_id=1, source_target_pairs={{0,1},{1,2},{2,3},{3,4},{4,5},{5,6},{6,7},{7,0},{8,9},{9,10},{10,1... | collective-permute-start | bytes 602120 | tf_op jit(solution)/shard_map/ppermute | solution.py:15
  367.0 6.9 %collective-permute-start.10 = (bf16[1,112,896]{2,1,0:T(8,128)(2,1)S(1)}, bf16[1,112,896]{2,1,0:T(8,128)(2,1)S(1)}, u32[]{:S(2)}, u32[]{:S(2)}) collective-permute-start(bf16[1,112,896]{2,1,0:T(8,128)(2,1)S(1)} %collective-permute-done.9), channel_id=1, source_target_pairs={{0,1},{1,2},{2,3},{3,4},{4,5},{5,6},{6,7},{7,0},{8,9},{9,10},{10,1... | collective-permute-start | bytes 602120 | tf_op jit(solution)/shard_map/ppermute | solution.py:15
  374.0 6.9 %collective-permute-start.11 = (bf16[1,112,896]{2,1,0:T(8,128)(2,1)S(1)}, bf16[1,112,896]{2,1,0:T(8,128)(2,1)S(1)}, u32[]{:S(2)}, u32[]{:S(2)}) collective-permute-start(bf16[1,112,896]{2,1,0:T(8,128)(2,1)S(1)} %collective-permute-done.10), channel_id=1, source_target_pairs={{0,1},{1,2},{2,3},{3,4},{4,5},{5,6},{6,7},{7,0},{8,9},{9,10},{10,1... | collective-permute-start | bytes 602120 | tf_op jit(solution)/shard_map/ppermute | solution.py:15
  380.9 6.9 %collective-permute-start.12 = (bf16[1,112,896]{2,1,0:T(8,128)(2,1)S(1)}, bf16[1,112,896]{2,1,0:T(8,128)(2,1)S(1)}, u32[]{:S(2)}, u32[]{:S(2)}) collective-permute-start(bf16[1,112,896]{2,1,0:T(8,128)(2,1)S(1)} %collective-permute-done.11), channel_id=1, source_target_pairs={{0,1},{1,2},{2,3},{3,4},{4,5},{5,6},{6,7},{7,0},{8,9},{9,10},{10,1... | collective-permute-start | bytes 602120 | tf_op jit(solution)/shard_map/ppermute | solution.py:15
  387.9 6.9 %collective-permute-start.13 = (bf16[1,112,896]{2,1,0:T(8,128)(2,1)S(1)}, bf16[1,112,896]{2,1,0:T(8,128)(2,1)S(1)}, u32[]{:S(2)}, u32[]{:S(2)}) collective-permute-start(bf16[1,112,896]{2,1,0:T(8,128)(2,1)S(1)} %collective-permute-done.12), channel_id=1, source_target_pairs={{0,1},{1,2},{2,3},{3,4},{4,5},{5,6},{6,7},{7,0},{8,9},{9,10},{10,1... | collective-permute-start | bytes 602120 | tf_op jit(solution)/shard_map/ppermute | solution.py:15
  394.8 6.9 %collective-permute-start.14 = (bf16[1,112,896]{2,1,0:T(8,128)(2,1)S(1)}, bf16[1,112,896]{2,1,0:T(8,128)(2,1)S(1)}, u32[]{:S(2)}, u32[]{:S(2)}) collective-permute-start(bf16[1,112,896]{2,1,0:T(8,128)(2,1)S(1)} %collective-permute-done.13), channel_id=1, source_target_pairs={{0,1},{1,2},{2,3},{3,4},{4,5},{5,6},{6,7},{7,0},{8,9},{9,10},{10,1... | collective-permute-start | bytes 602120 | tf_op jit(solution)/shard_map/ppermute | solution.py:15
  401.7 6.9 %collective-permute-start.15 = (bf16[1,112,896]{2,1,0:T(8,128)(2,1)S(1)}, bf16[1,112,896]{2,1,0:T(8,128)(2,1)S(1)}, u32[]{:S(2)}, u32[]{:S(2)}) collective-permute-start(bf16[1,112,896]{2,1,0:T(8,128)(2,1)S(1)} %collective-permute-done.14), channel_id=1, source_target_pairs={{0,1},{1,2},{2,3},{3,4},{4,5},{5,6},{6,7},{7,0},{8,9},{9,10},{10,1... | collective-permute-start | bytes 602120 | tf_op jit(solution)/shard_map/ppermute | solution.py:15
  411.5 40.2 %collective-permute-start.17 = (bf16[1,896,896]{2,1,0:T(8,128)(2,1)S(1)}, bf16[1,896,896]{2,1,0:T(8,128)(2,1)S(1)}, u32[]{:S(2)}, u32[]{:S(2)}) collective-permute-start(bf16[1,896,896]{2,1,0:T(8,128)(2,1)S(1)} %fusion.4), channel_id=1, source_target_pairs={{8,0},{16,8},{24,16},{9,1},{17,9},{25,17},{10,2},{18,10},{26,18},{... | collective-permute-start | bytes 4816904 | tf_op jit(solution)/shard_map/ppermute | solution.py:29
  412.8 38.9 %collective-permute-start.16 = (bf16[1,896,896]{2,1,0:T(8,128)(2,1)S(1)}, bf16[1,896,896]{2,1,0:T(8,128)(2,1)S(1)}, u32[]{:S(2)}, u32[]{:S(2)}) collective-permute-start(bf16[1,896,896]{2,1,0:T(8,128)(2,1)S(1)} %fusion.4), channel_id=1, source_target_pairs={{0,8},{8,16},{16,24},{1,9},{9,17},{17,25},{2,10},{10,18},{18,26},{... | collective-permute-start | bytes 4816904 | tf_op jit(solution)/shard_map/ppermute | solution.py:26
Sparse Core Ops, SparseCore 0:
  168.7 104.6 all-reduce.2
  472.0 104.5 all-reduce.4
